TPU v7x, 32 devices: a whole 2x2x4 slice. The times are simulated.
32 devices in a mesh: dp: 4 (over y, x), fsdp: 8 (over z, core).
Axes of the slice: x: 2, y: 2, z: 4, core: 2. Of those that a mesh axis runs over, the one named last changes fastest.
Arguments:
- tokens: bfloat16 [32768, 1024], P(('dp', 'fsdp')), may hold values from -6 to 6
- segment_ids: int32 [32, 1024], P(('dp', 'fsdp')), may hold values from 0 to 19, never falling along the last dimension, each value on 1 to 512 neighbouring positions
- expert_ids: int32 [32768, 1], P(('dp', 'fsdp')), may hold values from 0 to 1; in each aligned block of 1024 rows (0 to 1023, 1024 to 2047, ...) at most 640 rows name the same one
- ln1_gain: bfloat16 [1024], P(('dp', 'fsdp')), may hold values from 0.5 to 1.5
- ln1_bias: bfloat16 [1024], P(('dp', 'fsdp')), may hold values from -0.59765625 to 0.59765625
- qkv_weight: bfloat16 [1024, 3072], P(('dp', 'fsdp')), may hold values from -0.1875 to 0.1875
- query_bias: bfloat16 [1024], P(('dp', 'fsdp')), may hold values from -0.59765625 to 0.59765625
- value_bias: bfloat16 [1024], P(('dp', 'fsdp')), may hold values from -0.59765625 to 0.59765625
- out_weight: bfloat16 [1024, 1024], P(('dp', 'fsdp')), may hold values from -0.375 to 0.375
- out_bias: bfloat16 [1024], P(('dp', 'fsdp')), may hold values from -0.59765625 to 0.59765625
- ln2_gain: bfloat16 [1024], P(('dp', 'fsdp')), may hold values from 0.5 to 1.5
- ln2_bias: bfloat16 [1024], P(('dp', 'fsdp')), may hold values from -0.59765625 to 0.59765625
- up_weight: bfloat16 [1024, 2, 4096], P(('dp', 'fsdp')), may hold values from -0.1875 to 0.1875
- up_bias: bfloat16 [2, 4096], P(None, ('dp', 'fsdp')), may hold values from -0.59765625 to 0.59765625
- down_weight: bfloat16 [4096, 2, 1024], P(('dp', 'fsdp')), may hold values from -0.125 to 0.125
- down_bias: bfloat16 [2, 1024], P(None, ('dp', 'fsdp')), may hold values from -0.59765625 to 0.59765625
- cotangent: bfloat16 [32768, 1024], P(('dp', 'fsdp')), may hold values from -6 to 6
Outputs:
- block_out: bfloat16 [32768, 1024], P(('dp', 'fsdp'))
- input_grad: float32 [32768, 1024], P(('dp', 'fsdp'))
- ln1_gain_grad: float32 [1024], P(('dp', 'fsdp'))
- ln1_bias_grad: float32 [1024], P(('dp', 'fsdp'))
- qkv_weight_grad: float32 [1024, 3072], P(('dp', 'fsdp'))
- query_bias_grad: float32 [1024], P(('dp', 'fsdp'))
- value_bias_grad: float32 [1024], P(('dp', 'fsdp'))
- out_weight_grad: float32 [1024, 1024], P(('dp', 'fsdp'))
- out_bias_grad: float32 [1024], P(('dp', 'fsdp'))
- ln2_gain_grad: float32 [1024], P(('dp', 'fsdp'))
- ln2_bias_grad: float32 [1024], P(('dp', 'fsdp'))
- up_weight_grad: float32 [1024, 2, 4096], P(('dp', 'fsdp'))
- up_bias_grad: float32 [2, 4096], P(None, ('dp', 'fsdp'))
- down_weight_grad: float32 [4096, 2, 1024], P(('dp', 'fsdp'))
- down_bias_grad: float32 [2, 1024], P(None, ('dp', 'fsdp'))
Inputs may be any that keep to these rules, and one draw needn't show every extreme that they name: `segment_ids`: each device's 1024 tokens are one packed sequence; its segment numbers never fall. `expert_ids`: at most 640 of the tokens of one device name one expert, and some device's tokens name one expert exactly that often.
All inputs are finite; a program needn't handle non-finite values.
Results may differ from a plain program's by a relative error of at most 0.012.
Values may be sent and summed in bfloat16 or wider, within the bound.
No kernel may reach another device: no remote copies, remote signals or barrier semaphores. Data moves between devices by JAX's collectives and lax.ppermute only.
A program may use at most 512 MiB of HBM per device.

v0:
```python
import jax
import jax.numpy as jnp
from jax import lax
from jax.sharding import PartitionSpec as P

HEADS = 16
HEAD_DIM = 64
EXPERTS = 2
CAPACITY = 640
epsilon = 1e-05


def layer_norm(values, gain, shift):
    centre = values - jnp.mean(values, -1, keepdims=True)
    spread = jnp.mean(centre * centre, -1, keepdims=True)
    return centre * lax.rsqrt(spread + epsilon) * gain + shift


def shards(
    tokens,
    segment_ids,
    expert_ids,
    ln1_gain,
    ln1_bias,
    qkv_weight,
    query_bias,
    value_bias,
    out_weight,
    out_bias,
    ln2_gain,
    ln2_bias,
    up_weight,
    up_bias,
    down_weight,
    down_bias,
    cotangent,
):
    float_type = jnp.float32
    half_type = jnp.bfloat16
    attention_full = (
        lax.all_gather(qkv_weight, ("dp", "fsdp"), axis=0, tiled=True),
        lax.all_gather(out_weight, ("dp", "fsdp"), axis=0, tiled=True),
        lax.all_gather(ln1_gain, ("dp", "fsdp"), axis=0, tiled=True),
        lax.all_gather(ln1_bias, ("dp", "fsdp"), axis=0, tiled=True),
        lax.all_gather(query_bias, ("dp", "fsdp"), axis=0, tiled=True),
        lax.all_gather(value_bias, ("dp", "fsdp"), axis=0, tiled=True),
        lax.all_gather(out_bias, ("dp", "fsdp"), axis=0, tiled=True),
    )
    w_qkv, w_out, gain_one, shift_one, bias_query, bias_value, bias_out = attention_full
    row_count, width = tokens.shape
    scale = HEAD_DIM ** (-0.5)
    block_rows = min(512, row_count)
    block_starts = list(range(0, row_count, block_rows))
    inputs = tokens.astype(float_type)
    gain_first = gain_one.astype(float_type)
    shift_first = shift_one.astype(float_type)
    normed_one = layer_norm(inputs, gain_first, shift_first)
    normed_low = normed_one.astype(half_type)
    qkv_bias = jnp.concatenate([bias_query, jnp.zeros_like(bias_query), bias_value]).astype(
        float_type
    )
    qkv_low = (jnp.dot(normed_low, w_qkv, preferred_element_type=float_type) + qkv_bias).astype(
        half_type
    )
    queries = qkv_low[:, :width].reshape(row_count, HEADS, HEAD_DIM)
    keys_low = qkv_low[:, width : 2 * width].reshape(row_count, HEADS, HEAD_DIM)
    values_low = qkv_low[:, 2 * width :].reshape(row_count, HEADS, HEAD_DIM)
    positions = lax.iota(jnp.int32, row_count)
    segment_row = segment_ids[0]
    allowed = (positions[None, :] <= positions[:, None]) & (
        segment_row[None, :] == segment_row[:, None]
    )

    def masked_scores(start):
        query_block = queries[start : start + block_rows]
        raw = jnp.einsum("qhd,khd->hqk", query_block, keys_low, preferred_element_type=float_type)
        return jnp.where(allowed[start : start + block_rows][None], raw * scale, -1e30)

    total_pieces = []
    attended_pieces = []
    for start in block_starts:
        scores = masked_scores(start)
        top_score = jnp.max(scores, -1, keepdims=True)
        log_piece = top_score + jnp.log(jnp.sum(jnp.exp(scores - top_score), -1, keepdims=True))
        probs_low = jnp.exp(scores - log_piece).astype(half_type)
        total_pieces.append(log_piece)
        attended_pieces.append(
            jnp.einsum("hqk,khd->qhd", probs_low, values_low, preferred_element_type=float_type)
        )
    attended = jnp.concatenate(attended_pieces, 0)
    attended_low = attended.reshape(row_count, width).astype(half_type)
    projected = jnp.dot(attended_low, w_out, preferred_element_type=float_type) + bias_out.astype(
        float_type
    )
    middle = inputs + projected
    expert_full = (
        lax.all_gather(up_weight, ("dp", "fsdp"), axis=0, tiled=True),
        lax.all_gather(down_weight, ("dp", "fsdp"), axis=0, tiled=True),
        lax.all_gather(up_bias, ("dp", "fsdp"), axis=1, tiled=True),
        lax.all_gather(down_bias, ("dp", "fsdp"), axis=1, tiled=True),
        lax.all_gather(ln2_gain, ("dp", "fsdp"), axis=0, tiled=True),
        lax.all_gather(ln2_bias, ("dp", "fsdp"), axis=0, tiled=True),
    )
    w_up, w_down, bias_up, bias_down, gain_two, shift_two = expert_full
    gain_second = gain_two.astype(float_type)
    shift_second = shift_two.astype(float_type)
    normed_two = layer_norm(middle, gain_second, shift_second)
    normed_two_low = normed_two.astype(half_type)
    route_ids = expert_ids[:, 0]
    one_hot = (route_ids[:, None] == lax.iota(jnp.int32, EXPERTS)[None, :]).astype(jnp.int32)
    slot_index = jnp.sum((jnp.cumsum(one_hot, 0) - 1) * one_hot, 1)
    flat_slot = route_ids * CAPACITY + slot_index
    sender = jnp.full((EXPERTS * CAPACITY,), row_count, jnp.int32).at[flat_slot].set(positions)

    def dispatch(values):
        padded = jnp.concatenate([values, jnp.zeros((1, values.shape[1]), values.dtype)], 0)
        return padded[sender].reshape(EXPERTS, CAPACITY, values.shape[1])

    def combine(slotted):
        return slotted.reshape(EXPERTS * CAPACITY, slotted.shape[2])[flat_slot]

    expert_input = dispatch(normed_two_low)
    inner = (
        jnp.einsum("ecd,def->ecf", expert_input, w_up, preferred_element_type=float_type)
        + bias_up.astype(float_type)[:, None, :]
    )
    activated, pull_gelu = jax.vjp(jax.nn.gelu, inner)
    hidden_low = activated.astype(half_type)
    branch = (
        jnp.einsum("ecf,fed->ecd", hidden_low, w_down, preferred_element_type=float_type)
        + bias_down.astype(float_type)[:, None, :]
    )
    result = middle + combine(branch)
    block_out = result.astype(half_type)
    expert_back = (
        lax.all_gather(up_weight, ("dp", "fsdp"), axis=0, tiled=True),
        lax.all_gather(down_weight, ("dp", "fsdp"), axis=0, tiled=True),
        lax.all_gather(up_bias, ("dp", "fsdp"), axis=1, tiled=True),
        lax.all_gather(down_bias, ("dp", "fsdp"), axis=1, tiled=True),
        lax.all_gather(ln2_gain, ("dp", "fsdp"), axis=0, tiled=True),
        lax.all_gather(ln2_bias, ("dp", "fsdp"), axis=0, tiled=True),
    )
    w_up_back = expert_back[0]
    w_down_back = expert_back[1]
    grad_slots = dispatch(cotangent)
    down_grad = jnp.einsum(
        "ecf,ecd->fed", hidden_low, grad_slots, preferred_element_type=float_type
    )
    down_bias_grad = jnp.sum(grad_slots.astype(float_type), 1)
    hidden_grad = jnp.einsum(
        "ecd,fed->ecf", grad_slots, w_down_back, preferred_element_type=float_type
    )
    inner_grad = pull_gelu(hidden_grad)[0].astype(half_type)
    up_grad = jnp.einsum(
        "ecd,ecf->def", expert_input, inner_grad, preferred_element_type=float_type
    )
    up_bias_grad = jnp.sum(inner_grad.astype(float_type), 1)
    normed_two_grad = combine(
        jnp.einsum("ecf,def->ecd", inner_grad, w_up_back, preferred_element_type=float_type)
    )
    ignored_two, pull_two = jax.vjp(layer_norm, middle, gain_second, shift_second)
    middle_part, gain_two_grad, shift_two_grad = pull_two(normed_two_grad)
    middle_grad = cotangent.astype(float_type) + middle_part
    expert_sums = (
        lax.psum_scatter(up_grad, ("dp", "fsdp"), scatter_dimension=0, tiled=True),
        lax.psum_scatter(up_bias_grad, ("dp", "fsdp"), scatter_dimension=1, tiled=True),
        lax.psum_scatter(down_grad, ("dp", "fsdp"), scatter_dimension=0, tiled=True),
        lax.psum_scatter(down_bias_grad, ("dp", "fsdp"), scatter_dimension=1, tiled=True),
        lax.psum_scatter(gain_two_grad, ("dp", "fsdp"), scatter_dimension=0, tiled=True),
        lax.psum_scatter(shift_two_grad, ("dp", "fsdp"), scatter_dimension=0, tiled=True),
    )
    attention_back = (
        lax.all_gather(qkv_weight, ("dp", "fsdp"), axis=0, tiled=True),
        lax.all_gather(out_weight, ("dp", "fsdp"), axis=0, tiled=True),
        lax.all_gather(ln1_gain, ("dp", "fsdp"), axis=0, tiled=True),
        lax.all_gather(ln1_bias, ("dp", "fsdp"), axis=0, tiled=True),
        lax.all_gather(query_bias, ("dp", "fsdp"), axis=0, tiled=True),
        lax.all_gather(value_bias, ("dp", "fsdp"), axis=0, tiled=True),
        lax.all_gather(out_bias, ("dp", "fsdp"), axis=0, tiled=True),
    )
    w_qkv_back = attention_back[0]
    w_out_back = attention_back[1]
    projected_grad = middle_grad.astype(half_type)
    out_grad = jnp.einsum(
        "td,te->de", attended_low, projected_grad, preferred_element_type=float_type
    )
    out_bias_grad = jnp.sum(projected_grad.astype(float_type), 0)
    attended_grad = jnp.einsum(
        "te,de->td", projected_grad, w_out_back, preferred_element_type=float_type
    )
    attended_grad = attended_grad.astype(half_type).reshape(row_count, HEADS, HEAD_DIM)
    values_grad = jnp.zeros((row_count, HEADS, HEAD_DIM), float_type)
    keys_grad = jnp.zeros((row_count, HEADS, HEAD_DIM), float_type)
    query_pieces = []
    for number, start in enumerate(block_starts):
        probs = jnp.exp(masked_scores(start) - total_pieces[number])
        probs_again = probs.astype(half_type)
        grad_block = attended_grad[start : start + block_rows]
        query_block = queries[start : start + block_rows]
        probs_grad = jnp.einsum(
            "qhd,khd->hqk", grad_block, values_low, preferred_element_type=float_type
        )
        values_grad = values_grad + jnp.einsum(
            "hqk,qhd->khd", probs_again, grad_block, preferred_element_type=float_type
        )
        score_grad = probs * (probs_grad - jnp.sum(probs_grad * probs, -1, keepdims=True))
        score_low = (score_grad * scale).astype(half_type)
        query_pieces.append(
            jnp.einsum("hqk,khd->qhd", score_low, keys_low, preferred_element_type=float_type)
        )
        keys_grad = keys_grad + jnp.einsum(
            "hqk,qhd->khd", score_low, query_block, preferred_element_type=float_type
        )
    queries_grad = jnp.concatenate(query_pieces, 0)
    qkv_grad = jnp.concatenate(
        [
            queries_grad.reshape(row_count, width),
            keys_grad.reshape(row_count, width),
            values_grad.reshape(row_count, width),
        ],
        1,
    ).astype(half_type)
    qkv_weight_grad = jnp.einsum(
        "td,te->de", normed_low, qkv_grad, preferred_element_type=float_type
    )
    column_sums = jnp.sum(qkv_grad.astype(float_type), 0)
    query_bias_grad = column_sums[:width]
    value_bias_grad = column_sums[2 * width :]
    normed_one_grad = jnp.einsum(
        "te,de->td", qkv_grad, w_qkv_back, preferred_element_type=float_type
    )
    ignored_one, pull_one = jax.vjp(layer_norm, inputs, gain_first, shift_first)
    input_part, gain_one_grad, shift_one_grad = pull_one(normed_one_grad)
    input_grad = middle_grad + input_part
    attention_sums = (
        lax.psum_scatter(qkv_weight_grad, ("dp", "fsdp"), scatter_dimension=0, tiled=True),
        lax.psum_scatter(out_grad, ("dp", "fsdp"), scatter_dimension=0, tiled=True),
        lax.psum_scatter(gain_one_grad, ("dp", "fsdp"), scatter_dimension=0, tiled=True),
        lax.psum_scatter(shift_one_grad, ("dp", "fsdp"), scatter_dimension=0, tiled=True),
        lax.psum_scatter(query_bias_grad, ("dp", "fsdp"), scatter_dimension=0, tiled=True),
        lax.psum_scatter(value_bias_grad, ("dp", "fsdp"), scatter_dimension=0, tiled=True),
        lax.psum_scatter(out_bias_grad, ("dp", "fsdp"), scatter_dimension=0, tiled=True),
    )
    return (
        block_out,
        input_grad,
        attention_sums[2],
        attention_sums[3],
        attention_sums[0],
        attention_sums[4],
        attention_sums[5],
        attention_sums[1],
        attention_sums[6],
        expert_sums[4],
        expert_sums[5],
        expert_sums[0],
        expert_sums[1],
        expert_sums[2],
        expert_sums[3],
    )


def solution(mesh):
    in_specs = (
        P(("dp", "fsdp"), None),
        P(("dp", "fsdp"), None),
        P(("dp", "fsdp"), None),
        P(("dp", "fsdp")),
        P(("dp", "fsdp")),
        P(("dp", "fsdp"), None),
        P(("dp", "fsdp")),
        P(("dp", "fsdp")),
        P(("dp", "fsdp"), None),
        P(("dp", "fsdp")),
        P(("dp", "fsdp")),
        P(("dp", "fsdp")),
        P(("dp", "fsdp"), None, None),
        P(None, ("dp", "fsdp")),
        P(("dp", "fsdp"), None, None),
        P(None, ("dp", "fsdp")),
        P(("dp", "fsdp"), None),
    )
    out_specs = (
        P(("dp", "fsdp"), None),
        P(("dp", "fsdp"), None),
        P(("dp", "fsdp")),
        P(("dp", "fsdp")),
        P(("dp", "fsdp"), None),
        P(("dp", "fsdp")),
        P(("dp", "fsdp")),
        P(("dp", "fsdp"), None),
        P(("dp", "fsdp")),
        P(("dp", "fsdp")),
        P(("dp", "fsdp")),
        P(("dp", "fsdp"), None, None),
        P(None, ("dp", "fsdp")),
        P(("dp", "fsdp"), None, None),
        P(None, ("dp", "fsdp")),
    )
    return jax.shard_map(shards, mesh=mesh, in_specs=in_specs, out_specs=out_specs, check_vma=False)
```

profile of v0, /device:TPU:0, one launch (start us, length us, event | category | flops | bytes accessed | tf_op | source)
XLA Modules:
  0.0 1819.6 jit_solution(12890577069319250570)
XLA Ops:
  8.7 2.1 copy.76
  10.9 2.0 copy.77
  14.6 1.8 concatenate.28
  18.5 4.3 scatter_custom_fusion
  22.9 5.1 gather_fusion.2
  28.0 2.3 convert_reduce_fusion.3
  33.2 43.4 %all-reduce.18 = (bf16[1024]{0:T(1024)(128)(2,1)S(1)}, bf16[1024]{0:T(1024)(128)(2,1)S(1)}, bf16[1024]{0:T(1024)(128)(2,1)S(1)}, bf16[1024]{0:T(1024)(128)(2,1)S...) all-reduce(bf16[1024]{0:T(1024)(128)(2,1)S(1)} %dynamic-update-slic, ...), channel_id=1, replica_groups=mesh['dp'=4,'fsdp'=8] {'dp','fsdp'}, use_global_device_ids=true, to_apply=%add.6 | all-reduce | flops 7168 | bytes 28672
  76.7 1.9 convert_reduce_fusion.2
  78.6 2.4 fusion.72
  81.6 39.9 %all_gather.53 = bf16[2,4096]{1,0:T(2,128)(2,1)S(1)} all-gather(bf16[2,128]{1,0:T(2,128)(2,1)S(1)} %copy-done.59), channel_id=1, replica_groups=mesh['dp'=4,'fsdp'=8] {'dp','fsdp'}, dimensions={1}, use_global_device_ids=true | all-gather | bytes 16896 | tf_op jit(solution)/shard_map/all_gather | solution.py:99
  123.2 10.3 add_convert_fusion
  133.5 1.5 fusion.140
  135.0 2.4 fusion.141
  137.5 2.9 copy.74
  140.4 2.2 copy.73
  142.6 2.7 copy.75
  145.2 3.9 copy.72
  149.2 15.5 fusion.5
  164.7 14.2 fusion.4
  178.9 25.7 %exponential_reduce_fusion = (f32[16,512]{1,0:T(8,128)S(1)}, f32[16,512]{1,0:T(8,128)S(1)}) fusion(f32[16,512,1024]{2,1,0:T(8,128)} %get-tuple-element.114, f32[16,512]{1,0:T(8,128)S(1)} %get-tuple-element.113, pred[512,1024]{1,0:T(8,128)(4,1)S(1)} %copy-done.16, f32[16,512]{1,0:T(8,128)S(1)} %get-tuple-element.115, f32[16,512,1024]{2,1,0:T(8,128)} %get-tuple-element.116, ...), kind=kLoop, calls=%fused_computation.14 | loop fusion | flops 67092480 | bytes 68288512 | tf_op jit(solution)/shard_map/reduce_sum | solution.py:84
  204.7 17.6 fusion.90
  222.3 15.7 fusion.91
  238.0 2.1 pad_maximum_fusion.1
  240.2 5.6 fusion.145
  248.8 5.1 gather_fusion
  253.8 4.9 all-gather.10.cloned.1.call-done
  258.7 19.5 %fusion.146 = f32[2,640,4096]{2,1,0:T(8,128)} fusion(bf16[2,640,1024]{2,1,0:T(8,128)(2,1)} %bitcast.116, bf16[1024,2,4096]{2,0,1:T(8,128)(2,1)} %all-gather.10.cloned.1.call-done), kind=kOutput, calls=%fused_computation.161 | convolution fusion | flops 10737418240 | bytes 40370176 | tf_op jit(solution)/shard_map/ecd,def->ecf/dot_general | solution.py:124
  278.1 96.4 %all-gather.12.cloned.1.call-done = bf16[4096,2,1024]{2,0,1:T(8,128)(2,1)} async-done(((bf16[128,2,1024]{2,0,1:T(8,128)(2,1)}), bf16[4096,2,1024]{2,0,1:T(8,128)(2,1)}) %all-gather.12.cloned.1.call-update) | async-done | bytes 16777232 | tf_op jit(solution)/shard_map/all_gather | solution.py:98
  374.6 29.6 %convert_reduce_fusion = (f32[2,4096]{1,0:T(2,128)S(1)}, bf16[2,640,4096]{2,1,0:T(8,128)(2,1)}) fusion(f32[2,640,4096]{2,1,0:T(8,128)} %fusion.146, f32[2,4096]{1,0:T(2,128)S(1)} %convert_element_type.108, bf16[2,640,1024]{2,1,0:T(8,128)(2,1)S(1)} %bitcast.102, bf16[4096,2,1024]{2,0,1:T(8,128)(2,1)} %all-gather.12.cloned.1.call-done), kind=kOutput, calls=%fused_computation.30 | convolution fusion | flops 10857996288 | bytes 50921472 | tf_op jit(solution)/shard_map/ecd,fed->ecf/dot_general | solution.py:150
  404.2 2.0 copy.85
  406.2 22.7 %convolution_bitcast_fusion = f32[1024,2,4096]{0,2,1:T(8,128)} fusion(bf16[2,640,4096]{2,1,0:T(8,128)(2,1)} %get-tuple-element.97, bf16[2,640,1024]{2,1,0:T(8,128)(2,1)} %bitcast.117), kind=kOutput, calls=%fused_computation.54 | convolution fusion | flops 10737418240 | bytes 46661632 | tf_op jit(solution)/shard_map/ecd,ecf->def/dot_general | solution.py:154
  429.0 49.3 %copy.80 = f32[1024,2,4096]{2,1,0:T(2,128)} copy(f32[1024,2,4096]{0,2,1:T(8,128)} %convolution_bitcast_fusion) | data formatting | bytes 67108864 | tf_op jit(solution)/shard_map/ecd,ecf->def/transpose | solution.py:154
  478.4 25.4 %convolution_bitcast_fusion.1 = f32[4096,2,1024]{0,2,1:T(8,128)} fusion(bf16[2,640,1024]{2,1,0:T(8,128)(2,1)S(1)} %bitcast.103, f32[2,640,4096]{2,1,0:T(8,128)} %fusion.146, f32[2,4096]{1,0:T(2,128)S(1)} %convert_element_type.108), kind=kOutput, calls=%fused_computation.55 | convolution fusion | flops 10789847040 | bytes 57180160 | tf_op jit(solution)/shard_map/ecf,ecd->fed/dot_general | solution.py:146
  504.4 38.4 %all-gather = bf16[32,32,2]{1,2,0:T(2,128)(2,1)S(1)} all-gather(bf16[1,32,2]{1,2,0:T(2,128)(2,1)S(1)} %bitcast.137), channel_id=1, replica_groups=mesh['dp'=4,'fsdp'=8] {'dp','fsdp'}, dimensions={0}, use_global_device_ids=true | all-gather | bytes 4224 | tf_op jit(solution)/shard_map/all_gather | solution.py:100
  543.0 19.3 %fusion.147 = f32[2,640,1024]{2,1,0:T(8,128)} fusion(bf16[2,640,4096]{2,1,0:T(8,128)(2,1)} %get-tuple-element.97, bf16[1024,2,4096]{2,0,1:T(8,128)(2,1)} %all-gather.10.cloned.1.call-done), kind=kOutput, calls=%fused_computation.162 | convolution fusion | flops 10737418240 | bytes 32505856 | tf_op jit(solution)/shard_map/ecf,def->ecd/dot_general | solution.py:159
  562.3 8.8 gather_fusion.3
  571.2 24.0 %broadcast_add_fusion = f32[2,640,1024]{2,1,0:T(8,128)} fusion(f32[2,1024]{1,0:T(2,128)S(1)} %bitcast.135, bf16[4096,2,1024]{2,0,1:T(8,128)(2,1)} %all-gather.12.cloned.1.call-done, f32[2,640,4096]{2,1,0:T(8,128)} %fusion.146, f32[2,4096]{1,0:T(2,128)S(1)} %convert_element_type.108), kind=kOutput, calls=%fused_computation.89 | convolution fusion | flops 10791157760 | bytes 43032576 | tf_op jit(solution)/shard_map/ecf,fed->ecd/dot_general | solution.py:130
  595.2 8.9 gather_fusion.1
  604.2 5.6 multiply_reduce_fusion.2
  610.1 4.8 fusion.139
  616.2 1.8 copy-done.61
  618.1 2.4 convolution_convert_fusion
  621.6 13.2 fusion.149
  634.8 59.4 %fusion.87 = bf16[512,16,64]{0,2,1:T(8,128)(2,1)} fusion(bf16[1024,16,64]{0,2,1:T(8,128)(2,1)S(1)} %bitcast.95, f32[16,512,1024]{2,1,0:T(8,128)} %fusion.149, f32[16,512,1024]{2,1,0:T(8,128)} %get-tuple-element.114, f32[16,512]{1,0:T(8,128)S(1)} %copy-done.48, pred[512,1024]{1,0:T(8,128)(4,1)} %get-tuple-element.110), kind=kOutput, calls=%fused_computation.98 | convolution fusion | flops 1166550016 | bytes 70811648 | tf_op jit(solution)/shard_map/hqk,khd->qhd/dot_general | solution.py:209
  694.1 6.9 fusion.150
  701.2 15.8 fusion.148
  717.0 62.9 %fusion.84 = bf16[512,16,64]{0,2,1:T(8,128)(2,1)} fusion(bf16[1024,16,64]{0,2,1:T(8,128)(2,1)S(1)} %bitcast.96, f32[16,512,1024]{2,1,0:T(8,128)} %fusion.148, f32[16,512,1024]{2,1,0:T(8,128)} %get-tuple-element.116, f32[16,512]{1,0:T(8,128)S(1)} %copy-done.50, pred[512,1024]{1,0:T(8,128)(4,1)} %get-tuple-element.109), kind=kOutput, calls=%fused_computation.97 | convolution fusion | flops 1166550016 | bytes 70811648 | tf_op jit(solution)/shard_map/hqk,khd->qhd/dot_general | solution.py:209
  779.8 3.2 pad_maximum_fusion.2
  783.0 61.5 %fusion.19 = f32[16,64,1024]{2,1,0:T(8,128)} fusion(bf16[512,16,64]{0,2,1:T(8,128)(2,1)S(1)} %bitcast.105, f32[16,512,1024]{2,1,0:T(8,128)} %fusion.148, f32[16,512,1024]{2,1,0:T(8,128)} %get-tuple-element.116, f32[16,512]{1,0:T(8,128)S(1)} %copy-done.50, pred[512,1024]{1,0:T(8,128)(4,1)} %get-tuple-element.109), kind=kOutput, calls=%fused_computation.33 | convolution fusion | flops 1166025728 | bytes 72908800 | tf_op jit(solution)/shard_map/hqk,qhd->khd/dot_general | solution.py:211
  844.6 60.4 %add_convert_fusion.2 = bf16[16,64,1024]{2,1,0:T(8,128)(2,1)} fusion(f32[16,64,1024]{2,1,0:T(8,128)} %fusion.19, bf16[512,16,64]{0,2,1:T(8,128)(2,1)S(1)} %bitcast.107, f32[16,512,1024]{2,1,0:T(8,128)} %fusion.149, f32[16,512,1024]{2,1,0:T(8,128)} %get-tuple-element.114, f32[16,512]{1,0:T(8,128)S(1)} %copy-done.48, pred[512,1024]{1,0:T(8,128)(4,1)} %get-tuple-element.110), kind=kOutput, calls=%fused_computation.80 | convolution fusion | flops 1168122880 | bytes 75005952 | tf_op jit(solution)/shard_map/hqk,qhd->khd/dot_general | solution.py:211
  905.0 17.6 fusion.94
  922.6 19.9 %add_convert_fusion.1 = bf16[16,64,1024]{2,1,0:T(8,128)(2,1)} fusion(f32[16,64,1024]{2,1,0:T(8,128)} %fusion.94, bf16[512,16,64]{0,2,1:T(8,128)(2,1)} %bitcast.113, f32[16,512,1024]{2,1,0:T(8,128)} %get-tuple-element.114, f32[16,512]{1,0:T(8,128)S(1)} %copy-done.48, pred[512,1024]{1,0:T(8,128)(4,1)S(1)} %copy-done.18), kind=kOutput, calls=%fused_computation.79 | convolution fusion | flops 1109393408 | bytes 41451520 | tf_op jit(solution)/shard_map/hqk,qhd->khd/dot_general | solution.py:203
  942.5 14.6 fusion.131
  958.6 11.7 fusion.136
  970.4 4.8 convert_reduce_fusion.1
  975.2 2.3 fusion.71
  977.5 40.5 %all-reduce.17 = (f32[1024]{0:T(1024)S(1)}, f32[1024]{0:T(1024)S(1)}, f32[1024]{0:T(1024)S(1)}, f32[1024]{0:T(1024)S(1)}, f32[1024]{0:T(1024)S(1)}, /*index=5*/f32[1024]{0:T(1024)S(1)}, f32[1024]{0:T(1024)S(1)}) all-reduce(f32[1024]{0:T(1024)S(1)} %get-tuple-element.77, ...), channel_id=2, replica_groups=mesh['dp'=4,'fsdp'=8] {'dp','fsdp'}, use_global_device_ids=true, to_apply=%region_19.20.clone | all-reduce | flops 7168 | bytes 57344
  1022.1 6.8 add_add_fusion.2
  1030.4 117.0 %all-reduce.21.cloned.1.call-done = f32[1024,2,4096]{2,1,0:T(2,128)} async-done(((f32[1024,2,4096]{2,1,0:T(2,128)}), f32[1024,2,4096]{2,1,0:T(2,128)}) %all-reduce.21.cloned.1.call-update) | async-done | bytes 33554448
  1147.4 2.3 constant_dynamic-slice_fusion
  1149.7 360.8 %reduce-scatter.14.cloned.1.call-done = f32[128,2,1024]{0,2,1:T(8,128)} async-done(((f32[4096,2,1024]{0,2,1:T(8,128)}), f32[128,2,1024]{0,2,1:T(8,128)}) %reduce-scatter.14.cloned.1.call-update) | async-done | bytes 1048592 | tf_op jit(solution)/shard_map/reduce_scatter | solution.py:167
  1510.5 2.3 copy.82
  1512.8 139.9 %reduce-scatter.12.cloned.1.call-done = f32[32,1024]{1,0:T(8,128)} async-done(((f32[1024,1024]{1,0:T(8,128)}), f32[32,1024]{1,0:T(8,128)}) %reduce-scatter.12.cloned.1.call-update) | async-done | bytes 131088 | tf_op jit(solution)/shard_map/reduce_scatter | solution.py:237
  1652.7 159.6 %reduce-scatter.10.cloned.1.call-done = f32[32,3072]{1,0:T(8,128)} async-done(((f32[1024,3072]{1,0:T(8,128)}), f32[32,3072]{1,0:T(8,128)}) %reduce-scatter.10.cloned.1.call-update) | async-done | bytes 393232 | tf_op jit(solution)/shard_map/reduce_scatter | solution.py:236
  (224 shorter events, 24.1 us)
Async XLA Ops:
  7.2 116.0 %all-gather.6.cloned.1.call-start = ((), (), s32[]{:S(2)}) async-start(), calls=%async_computation.5 | async-start | bytes 6488064 | tf_op jit(solution)/shard_map/all_gather | solution.py:41
  7.9 232.3 %all-gather.8.cloned.1.call-start = ((), (), s32[]{:S(2)}) async-start(), calls=%async_computation.6 | async-start | bytes 2162688 | tf_op jit(solution)/shard_map/all_gather | solution.py:42
  8.7 250.0 %all-gather.10.cloned.1.call-start = ((), (), s32[]{:S(2)}) async-start(), calls=%async_computation.7 | async-start | bytes 17301504 | tf_op jit(solution)/shard_map/all_gather | solution.py:97
  10.9 363.7 %all-gather.12.cloned.1.call-start = ((), (), s32[]{:S(2)}) async-start(), calls=%async_computation.8 | async-start | bytes 17301504 | tf_op jit(solution)/shard_map/all_gather | solution.py:98
  12.9 944.3 %reduce-scatter.18.cloned.1.call-start = ((), (), s32[]{:S(2)}) async-start(), calls=%async_computation.13 | async-start | bytes 540672
  22.8 8.7 copy-start.62
  22.8 8.9 copy-start.63
  22.8 9.1 copy-start.64
  22.9 9.4 copy-start.65
  22.9 9.6 copy-start.66
  22.9 9.8 copy-start.67
  22.9 10.0 copy-start.68
  22.9 58.7 %copy-start.59 = (bf16[2,128]{1,0:T(2,128)(2,1)S(1)}, bf16[2,128]{1,0:T(2,128)(2,1)}, u32[]{:S(2)}) copy-start(bf16[2,128]{1,0:T(2,128)(2,1)} %param.30) | copy-start | bytes 1540
  22.9 98.6 %copy-start.54 = (s32[1,1024]{1,0:T(1,128)S(1)}, s32[1,1024]{1,0:T(1,128)}, u32[]{:S(2)}) copy-start(s32[1,1024]{1,0:T(1,128)} %param.18) | copy-start | bytes 12292
  28.0 95.1 %copy-start.8 = (bf16[1024,1024]{1,0:T(8,128)(2,1)S(1)}, bf16[1024,1024]{1,0:T(8,128)(2,1)}, u32[]{:S(2)}) copy-start(bf16[1024,1024]{1,0:T(8,128)(2,1)} %param.17) | copy-start | bytes 6291460
  31.4 997.5 %reduce-scatter.16.cloned.1.call-start = ((), (), s32[]{:S(2)}) async-start(), calls=%async_computation.12 | async-start | bytes 2162688
  76.6 56.9 %copy-start.39 = (f32[1024]{0:T(1024)}, f32[1024]{0:T(1024)S(1)}, u32[]{:S(2)}) copy-start(f32[1024]{0:T(1024)S(1)} %convert_element_type.95) | copy-start | bytes 12292
  76.6 170.8 %copy-start.31 = (f32[1024]{0:T(1024)}, f32[1024]{0:T(1024)S(1)}, u32[]{:S(2)}) copy-start(f32[1024]{0:T(1024)S(1)} %convert_element_type.104) | copy-start | bytes 12292
  76.6 56.9 %copy-start.57 = (f32[1024]{0:T(1024)}, f32[1024]{0:T(1024)S(1)}, u32[]{:S(2)}) copy-start(f32[1024]{0:T(1024)S(1)} %convert_element_type.96) | copy-start | bytes 12292
  78.6 54.9 %copy-start.35 = (f32[1024]{0:T(1024)}, f32[1024]{0:T(1024)S(1)}, u32[]{:S(2)}) copy-start(f32[1024]{0:T(1024)S(1)} %broadcast_multiply_fusion.1) | copy-start | bytes 12292
  81.6 51.9 %copy-start.41 = (f32[1024]{0:T(1024)}, f32[1024]{0:T(1024)S(1)}, u32[]{:S(2)}) copy-start(f32[1024]{0:T(1024)S(1)} %fusion.101) | copy-start | bytes 12292
  140.4 24.4 %copy-start.2 = (bf16[1024,1024]{0,1:T(8,128)(2,1)}, bf16[1024,1024]{0,1:T(8,128)(2,1)S(1)}, u32[]{:S(2)}) copy-start(bf16[1024,1024]{0,1:T(8,128)(2,1)S(1)} %copy.74) | copy-start | bytes 6291460
  142.6 22.1 %copy-start.13 = (bf16[512,1024]{0,1:T(8,128)(2,1)}, bf16[512,1024]{0,1:T(8,128)(2,1)S(1)}, u32[]{:S(2)}) copy-start(bf16[512,1024]{0,1:T(8,128)(2,1)S(1)} %copy.73) | copy-start | bytes 3145732
  149.2 15.5 copy-start.19
  164.7 14.2 copy-start.16
  178.9 25.7 %copy-start.4 = (bf16[1024,1024]{0,1:T(8,128)(2,1)S(1)}, bf16[1024,1024]{0,1:T(8,128)(2,1)}, u32[]{:S(2)}) copy-start(bf16[1024,1024]{0,1:T(8,128)(2,1)} %copy.72) | copy-start | bytes 6291460
  178.9 25.7 %copy-start.20 = (pred[512,1024]{1,0:T(8,128)(4,1)S(1)}, pred[512,1024]{1,0:T(8,128)(4,1)}, u32[]{:S(2)}) copy-start(pred[512,1024]{1,0:T(8,128)(4,1)} %get-tuple-element.109) | copy-start | bytes 1572868
  204.6 17.7 copy-start.47
  204.7 17.7 copy-start.49
  204.7 17.7 copy-start.17
  240.1 5.7 copy-start.26
  258.7 115.9 %copy-start.12 = (bf16[1280,1024]{1,0:T(8,128)(2,1)S(1)}, bf16[1280,1024]{1,0:T(8,128)(2,1)}, u32[]{:S(2)}) copy-start(bf16[1280,1024]{1,0:T(8,128)(2,1)} %gather_fusion.2) | copy-start | bytes 7864324
  406.2 741.2 %all-reduce.21.cloned.1.call-start = ((), (), s32[]{:S(2)}) async-start(), calls=%async_computation.14 | async-start | bytes 67108864
  478.3 1032.2 %reduce-scatter.14.cloned.1.call-start = ((), (), s32[]{:S(2)}) async-start(), calls=%async_computation.11 | async-start | bytes 34603008 | tf_op jit(solution)/shard_map/reduce_scatter | solution.py:167
  503.8 39.2 %copy-start.56 = (s32[1024,1]{0,1:T(1,128)S(1)}, s32[1024,1]{0,1:T(1,128)}, u32[]{:S(2)}) copy-start(s32[1024,1]{0,1:T(1,128)} %copy-done.55) | copy-start | bytes 12292
  503.8 1148.8 %reduce-scatter.12.cloned.1.call-start = ((), (), s32[]{:S(2)}) async-start(), calls=%async_computation.10 | async-start | bytes 4325376 | tf_op jit(solution)/shard_map/reduce_scatter | solution.py:237
  595.2 9.0 copy-start.30
  595.2 9.0 copy-start.32
  595.2 9.0 copy-start.34
  604.1 5.6 copy-start.46
  604.2 5.6 copy-start.1
  604.2 5.9 copy-start.7
  620.6 80.5 %copy-start.24 = (bf16[512,1024]{0,1:T(8,128)(2,1)}, bf16[512,1024]{0,1:T(8,128)(2,1)S(1)}, u32[]{:S(2)}) copy-start(bf16[512,1024]{0,1:T(8,128)(2,1)S(1)} %get-tuple-element.108) | copy-start | bytes 3145732
  621.6 13.2 copy-start.3
  621.6 13.2 copy-start.48
  701.1 1111.2 %reduce-scatter.10.cloned.1.call-start = ((), (), s32[]{:S(2)}) async-start(), calls=%async_computation.9 | async-start | bytes 12976128 | tf_op jit(solution)/shard_map/reduce_scatter | solution.py:236
  701.2 15.8 copy-start.50
  717.0 66.0 %copy-start.14 = (bf16[512,1024]{0,1:T(8,128)(2,1)S(1)}, bf16[512,1024]{0,1:T(8,128)(2,1)}, u32[]{:S(2)}) copy-start(bf16[512,1024]{0,1:T(8,128)(2,1)} %copy-done.13) | copy-start | bytes 3145732
  783.0 61.5 %copy-start.15 = (bf16[512,1024]{0,1:T(8,128)(2,1)S(1)}, bf16[512,1024]{0,1:T(8,128)(2,1)}, u32[]{:S(2)}) copy-start(bf16[512,1024]{0,1:T(8,128)(2,1)} %copy.75) | copy-start | bytes 3145732
  844.5 60.4 %copy-start.21 = (pred[512,1024]{1,0:T(8,128)(4,1)S(1)}, pred[512,1024]{1,0:T(8,128)(4,1)}, u32[]{:S(2)}) copy-start(pred[512,1024]{1,0:T(8,128)(4,1)} %get-tuple-element.109) | copy-start | bytes 1572868
  905.0 17.6 copy-start.18
  922.5 19.9 %copy-start.9 = (bf16[1024,1024]{1,0:T(8,128)(2,1)S(1)}, bf16[1024,1024]{1,0:T(8,128)(2,1)}, u32[]{:S(2)}) copy-start(bf16[1024,1024]{1,0:T(8,128)(2,1)} %param.17) | copy-start | bytes 6291460
  922.5 19.9 %copy-start.36 = (f32[1024]{0:T(1024)S(1)}, f32[1024]{0:T(1024)}, u32[]{:S(2)}) copy-start(f32[1024]{0:T(1024)} %copy-done.35) | copy-start | bytes 12292
  922.6 19.9 %copy-start.40 = (f32[1024]{0:T(1024)S(1)}, f32[1024]{0:T(1024)}, u32[]{:S(2)}) copy-start(f32[1024]{0:T(1024)} %copy-done.39) | copy-start | bytes 12292
  922.6 19.9 %copy-start.42 = (f32[1024]{0:T(1024)S(1)}, f32[1024]{0:T(1024)}, u32[]{:S(2)}) copy-start(f32[1024]{0:T(1024)} %copy-done.41) | copy-start | bytes 12292
  922.6 19.9 %copy-start.58 = (f32[1024]{0:T(1024)S(1)}, f32[1024]{0:T(1024)}, u32[]{:S(2)}) copy-start(f32[1024]{0:T(1024)} %copy-done.57) | copy-start | bytes 12292
  958.6 11.8 copy-start.44
  958.6 11.8 copy-start.22
  958.6 11.8 copy-start.27
  958.6 11.8 copy-start.28
  970.3 7.2 copy-start.51
  970.3 7.2 copy-start.52
  970.3 7.2 copy-start.53
  970.3 51.8 %copy-start.38 = (f32[1024]{0:T(1024)S(1)}, f32[1024]{0:T(1024)}, u32[]{:S(2)}) copy-start(f32[1024]{0:T(1024)} %copy-done.37) | copy-start | bytes 12292
  (15 other events, 41.2 us)
Sparse Core Ops, SparseCore 0:
  11.0 72.1 all-gather.5
  86.2 55.7 all-gather.7
  145.0 113.6 all-gather.9
  261.6 112.9 all-gather.11
  376.7 132.1 reduce-scatter.17
  511.1 133.0 reduce-scatter.15
  650.6 496.7 all-reduce.20
  1149.8 360.6 reduce-scatter.13
  1513.5 139.1 reduce-scatter.11
  1660.1 152.0 reduce-scatter.9
where the time goes:
time: 1830 us; the launch traced here: 1820 us
  waiting for transfers between devices  880 us (48%)
  matrix products  566 us (31%)
  blocking collectives  162 us (9%)
  local copies, waits for them, and re-layouts  127 us (7%)
  other arithmetic  68 us (4%)
    reduce_scatter x1, waiting for transfers between devices, shards(): lax.psum_scatter(down_grad, ('dp', 'fsdp'), scatter_dimension=0, tiled=True)  361 us
    reduce_scatter x1, waiting for transfers between devices, shards(): lax.psum_scatter(qkv_weight_grad, ('dp', 'fsdp'), scatter_dimension=0, ti...  160 us
    reduce_scatter x1, waiting for transfers between devices, shards(): lax.psum_scatter(out_grad, ('dp', 'fsdp'), scatter_dimension=0, tiled=True)  140 us
    dot_general x2, matrix products, shards(): jnp.einsum('hqk,khd->qhd', score_low, keys_low, preferred_element_type=fl...  122 us
    dot_general x2, matrix products, shards(): jnp.einsum('hqk,qhd->khd', score_low, query_block, preferred_element_type...  122 us
    unnamed x13, waiting for transfers between devices  119 us
    all_gather x1, waiting for transfers between devices, shards(): lax.all_gather(down_weight, ('dp', 'fsdp'), axis=0, tiled=True)  96.4 us
    unnamed x2, blocking collectives  84 us
  transfers between devices with their start and end apart: 10, of which 6 were waited for; matrix products, arithmetic and copies ran while one was open for 41% of the time, Pallas kernels for 0%

commit v1 on v0

--- a/solution.py
+++ b/solution.py
@@ -8,6 +8,18 @@
 EXPERTS = 2
 CAPACITY = 640
 epsilon = 1e-05
+
+
+def collect(array, axis, dim):
+    ways, here = (lax.axis_size(axis), lax.axis_index(axis))
+    grown, reach = (array, 1)
+    while reach < ways:
+        theirs = lax.ppermute(grown, axis, [(d, d ^ reach) for d in range(ways)])
+        mine_first = jnp.concatenate([grown, theirs], axis=dim)
+        theirs_first = jnp.concatenate([theirs, grown], axis=dim)
+        grown = jnp.where(here & reach == 0, mine_first, theirs_first)
+        reach = 2 * reach
+    return grown
 
 
 def layer_norm(values, gain, shift):
@@ -95,7 +107,7 @@
     middle = inputs + projected
     expert_full = (
         lax.all_gather(up_weight, ("dp", "fsdp"), axis=0, tiled=True),
-        lax.all_gather(down_weight, ("dp", "fsdp"), axis=0, tiled=True),
+        collect(down_weight, ("dp", "fsdp"), 0),
         lax.all_gather(up_bias, ("dp", "fsdp"), axis=1, tiled=True),
         lax.all_gather(down_bias, ("dp", "fsdp"), axis=1, tiled=True),
         lax.all_gather(ln2_gain, ("dp", "fsdp"), axis=0, tiled=True),

time: 1830 us -> 1930 us (1.055)
  other arithmetic: 68 us -> 210 us
  waiting for transfers between devices: 880 us -> 821 us
    ppermute x0 -> x5, waiting for transfers between devices: none -> 503 us  [collect(): theirs = lax.ppermute(grown, axis, [(d, d ^ reach) for d in range(ways)])]
    reduce_scatter x1, waiting for transfers between devices: 361 us -> 0.01 us  [shards(): lax.psum_scatter(down_grad, ('dp', 'fsdp'), scatter_dimension=0, tiled=True)]
    select_n x0 -> x5, other arithmetic: none -> 143 us  [collect(): grown = jnp.where(here & reach == 0, mine_first, theirs_first)]
    unnamed x13, waiting for transfers between devices: 119 us -> 1.53 us
    reduce_scatter x1, waiting for transfers between devices: 140 us -> 54.4 us  [shards(): lax.psum_scatter(out_grad, ('dp', 'fsdp'), scatter_dimension=0, tiled=True)]
  transfers between devices with their start and end apart: 10 -> 15, of which waited for: 6 -> 9; matrix products, arithmetic and copies ran while one was open for 41% -> 47% of each run, Pallas kernels for 0% -> 0%
where the time goes in v1:
time: 1930 us; the launch traced here: 1920 us
  waiting for transfers between devices  821 us (43%)
  matrix products  577 us (30%)
  other arithmetic  210 us (11%)
  blocking collectives  160 us (8%)
  local copies, waits for them, and re-layouts  128 us (7%)
    ppermute x5, waiting for transfers between devices, collect(): theirs = lax.ppermute(grown, axis, [(d, d ^ reach) for d in range(ways)])  503 us
    reduce_scatter x1, waiting for transfers between devices, shards(): lax.psum_scatter(qkv_weight_grad, ('dp', 'fsdp'), scatter_dimension=0, ti...  160 us
    select_n x5, other arithmetic, collect(): grown = jnp.where(here & reach == 0, mine_first, theirs_first)  143 us
    dot_general x2, matrix products, shards(): jnp.einsum('hqk,khd->qhd', score_low, keys_low, preferred_element_type=fl...  135 us
    dot_general x2, matrix products, shards(): jnp.einsum('hqk,qhd->khd', score_low, query_block, preferred_element_type...  121 us
    all_gather x1, waiting for transfers between devices, shards(): lax.all_gather(down_weight, ('dp', 'fsdp'), axis=0, tiled=True)  96.5 us
    unnamed x2, blocking collectives  81.3 us
    reduce_scatter x1, waiting for transfers between devices, shards(): lax.psum_scatter(out_grad, ('dp', 'fsdp'), scatter_dimension=0, tiled=True)  54.4 us
  transfers between devices with their start and end apart: 15, of which 9 were waited for; matrix products, arithmetic and copies ran while one was open for 47% of the time, Pallas kernels for 0%

profile of v1, /device:TPU:0, one launch (start us, length us, event | category | flops | bytes accessed | tf_op | source)
XLA Modules:
  0.0 1917.9 jit_solution(7839477021296297108)
XLA Ops:
  8.7 2.1 copy.79
  18.5 4.3 scatter_custom_fusion
  22.9 5.1 gather_fusion.2
  28.0 2.3 convert_reduce_fusion.3
  33.1 43.4 %all-reduce.18 = (bf16[1024]{0:T(1024)(128)(2,1)S(1)}, bf16[1024]{0:T(1024)(128)(2,1)S(1)}, bf16[1024]{0:T(1024)(128)(2,1)S(1)}, bf16[1024]{0:T(1024)(128)(2,1)S...) all-reduce(bf16[1024]{0:T(1024)(128)(2,1)S(1)} %dynamic-update-slic, ...), channel_id=1, replica_groups=mesh['dp'=4,'fsdp'=8] {'dp','fsdp'}, use_global_device_ids=true, to_apply=%add.6 | all-reduce | flops 7168 | bytes 28672
  78.6 2.4 fusion.74
  81.6 39.8 %all_gather.52 = bf16[2,4096]{1,0:T(2,128)(2,1)S(1)} all-gather(bf16[2,128]{1,0:T(2,128)(2,1)S(1)} %copy-done.60), channel_id=1, replica_groups=mesh['dp'=4,'fsdp'=8] {'dp','fsdp'}, dimensions={1}, use_global_device_ids=true | all-gather | bytes 16896 | tf_op jit(solution)/shard_map/all_gather | solution.py:111
  123.1 10.3 add_convert_fusion
  135.0 2.4 fusion.145
  137.4 2.9 copy.77
  140.3 2.2 copy.76
  142.5 2.7 copy.78
  145.2 4.0 copy.75
  149.1 15.5 fusion.5
  164.7 14.2 fusion.4
  178.9 25.7 %exponential_reduce_fusion = (f32[16,512]{1,0:T(8,128)S(1)}, f32[16,512]{1,0:T(8,128)S(1)}) fusion(f32[16,512,1024]{2,1,0:T(8,128)} %get-tuple-element.114, f32[16,512]{1,0:T(8,128)S(1)} %get-tuple-element.113, pred[512,1024]{1,0:T(8,128)(4,1)S(1)} %copy-done.16, f32[16,512]{1,0:T(8,128)S(1)} %get-tuple-element.115, f32[16,512,1024]{2,1,0:T(8,128)} %get-tuple-element.116, ...), kind=kLoop, calls=%fused_computation.14 | loop fusion | flops 67092480 | bytes 68288512 | tf_op jit(solution)/shard_map/reduce_sum | solution.py:96
  204.7 17.6 fusion.94
  222.3 15.7 fusion.95
  240.1 5.6 fusion.149
  248.7 5.1 gather_fusion
  253.8 4.8 all-gather.10.cloned.1.call-done
  258.6 19.4 %fusion.150 = f32[2,640,4096]{2,1,0:T(8,128)} fusion(bf16[2,640,1024]{2,1,0:T(8,128)(2,1)} %bitcast.115, bf16[1024,2,4096]{2,0,1:T(8,128)(2,1)} %all-gather.10.cloned.1.call-done), kind=kOutput, calls=%fused_computation.168 | convolution fusion | flops 10737418240 | bytes 40370176 | tf_op jit(solution)/shard_map/ecd,def->ecf/dot_general | solution.py:136
  278.0 96.5 %all-gather.12.cloned.1.call-done = bf16[4096,2,1024]{2,0,1:T(8,128)(2,1)} async-done(((bf16[128,2,1024]{2,0,1:T(8,128)(2,1)}), bf16[4096,2,1024]{2,0,1:T(8,128)(2,1)}) %all-gather.12.cloned.1.call-update) | async-done | bytes 16777232 | tf_op jit(solution)/shard_map/all_gather | solution.py:149
  374.5 29.7 %convert_reduce_fusion = (f32[2,4096]{1,0:T(2,128)S(1)}, bf16[2,640,4096]{2,1,0:T(8,128)(2,1)}) fusion(f32[2,640,4096]{2,1,0:T(8,128)} %fusion.150, f32[2,4096]{1,0:T(2,128)S(1)} %convert_element_type.108, bf16[2,640,1024]{2,1,0:T(8,128)(2,1)S(1)} %bitcast.101, bf16[4096,2,1024]{2,0,1:T(8,128)(2,1)} %all-gather.12.cloned.1.call-done), kind=kOutput, calls=%fused_computation.31 | convolution fusion | flops 10857996288 | bytes 50921472 | tf_op jit(solution)/shard_map/ecd,fed->ecf/dot_general | solution.py:162
  406.3 22.7 %convolution_bitcast_fusion = f32[1024,2,4096]{0,2,1:T(8,128)} fusion(bf16[2,640,4096]{2,1,0:T(8,128)(2,1)} %get-tuple-element.97, bf16[2,640,1024]{2,1,0:T(8,128)(2,1)} %bitcast.116), kind=kOutput, calls=%fused_computation.58 | convolution fusion | flops 10737418240 | bytes 46661632 | tf_op jit(solution)/shard_map/ecd,ecf->def/dot_general | solution.py:166
  429.0 49.4 %copy.84 = f32[1024,2,4096]{2,1,0:T(2,128)} copy(f32[1024,2,4096]{0,2,1:T(8,128)} %convolution_bitcast_fusion) | data formatting | bytes 67108864 | tf_op jit(solution)/shard_map/ecd,ecf->def/transpose | solution.py:166
  478.5 25.3 %convolution_bitcast_fusion.1 = f32[4096,2,1024]{0,2,1:T(8,128)} fusion(bf16[2,640,1024]{2,1,0:T(8,128)(2,1)S(1)} %bitcast.102, f32[2,640,4096]{2,1,0:T(8,128)} %fusion.150, f32[2,4096]{1,0:T(2,128)S(1)} %convert_element_type.108), kind=kOutput, calls=%fused_computation.59 | convolution fusion | flops 10789847040 | bytes 57180160 | tf_op jit(solution)/shard_map/ecf,ecd->fed/dot_general | solution.py:158
  506.7 2.8 broadcast_select_fusion.4
  510.1 29.5 %collective-permute-done.1 = bf16[256,2,1024]{2,1,0:T(2,128)(2,1)} collective-permute-done((bf16[256,2,1024]{2,1,0:T(2,128)(2,1)S(1)}, bf16[256,2,1024]{2,1,0:T(2,128)(2,1)}, u32[]{:S(2)}, u32[]{:S(2)}) %collective-permute-start.1) | collective-permute-done | bytes 1048608 | tf_op jit(solution)/shard_map/ppermute | solution.py:17
  539.6 5.8 broadcast_select_fusion.3
  547.0 103.9 %collective-permute-done.2 = bf16[512,2,1024]{2,1,0:T(2,128)(2,1)} collective-permute-done((bf16[512,2,1024]{2,1,0:T(2,128)(2,1)S(1)}, bf16[512,2,1024]{2,1,0:T(2,128)(2,1)}, u32[]{:S(2)}, u32[]{:S(2)}) %collective-permute-start.2) | collective-permute-done | bytes 2097184 | tf_op jit(solution)/shard_map/ppermute | solution.py:17
  650.8 11.4 broadcast_select_fusion.2
  664.3 142.1 %collective-permute-done.3 = bf16[1024,2,1024]{2,1,0:T(2,128)(2,1)} collective-permute-done((bf16[1024,2,1024]{2,1,0:T(2,128)(2,1)}, bf16[1024,2,1024]{2,1,0:T(2,128)(2,1)}, u32[]{:S(2)}, u32[]{:S(2)}) %collective-permute-start.3) | collective-permute-done | bytes 4194336 | tf_op jit(solution)/shard_map/ppermute | solution.py:17
  806.3 41.5 %broadcast_select_fusion.1 = bf16[2048,2,1024]{2,1,0:T(2,128)(2,1)} fusion(pred[]{:T(512)S(6)} %eq.68, bf16[1024,2,1024]{2,1,0:T(2,128)(2,1)} %collective-permute-done.3, bf16[1024,2,1024]{2,1,0:T(2,128)(2,1)} %broadcast_select_fusion.2), kind=kLoop, calls=%fused_computation.53 | loop fusion | flops 12582912 | bytes 16777216 | tf_op jit(solution)/shard_map/jit(_where)/select_n | solution.py:20
  849.3 38.4 %all-gather = bf16[32,32,2]{1,2,0:T(2,128)(2,1)S(1)} all-gather(bf16[1,32,2]{1,2,0:T(2,128)(2,1)S(1)} %bitcast.136), channel_id=1, replica_groups=mesh['dp'=4,'fsdp'=8] {'dp','fsdp'}, dimensions={0}, use_global_device_ids=true | all-gather | bytes 4224 | tf_op jit(solution)/shard_map/all_gather | solution.py:112
  887.8 226.0 %collective-permute-done.4 = bf16[2048,2,1024]{2,1,0:T(2,128)(2,1)} collective-permute-done((bf16[2048,2,1024]{2,1,0:T(2,128)(2,1)}, bf16[2048,2,1024]{2,1,0:T(2,128)(2,1)}, u32[]{:S(2)}, u32[]{:S(2)}) %collective-permute-start.4) | collective-permute-done | bytes 8388640 | tf_op jit(solution)/shard_map/ppermute | solution.py:17
  1113.8 81.2 %broadcast_select_fusion = bf16[4096,2,1024]{2,1,0:T(2,128)(2,1)} fusion(pred[]{:T(512)S(6)} %eq.67, bf16[2048,2,1024]{2,1,0:T(2,128)(2,1)} %collective-permute-done.4, bf16[2048,2,1024]{2,1,0:T(2,128)(2,1)} %broadcast_select_fusion.1), kind=kLoop, calls=%fused_computation.19 | loop fusion | flops 25165824 | bytes 33554432 | tf_op jit(solution)/shard_map/jit(_where)/select_n | solution.py:20
  1194.9 19.4 %fusion.151 = f32[2,640,1024]{2,1,0:T(8,128)} fusion(bf16[2,640,4096]{2,1,0:T(8,128)(2,1)} %get-tuple-element.97, bf16[1024,2,4096]{2,0,1:T(8,128)(2,1)} %all-gather.10.cloned.1.call-done), kind=kOutput, calls=%fused_computation.169 | convolution fusion | flops 10737418240 | bytes 32505856 | tf_op jit(solution)/shard_map/ecf,def->ecd/dot_general | solution.py:171
  1214.3 8.9 gather_fusion.3
  1223.2 24.8 %broadcast_add_fusion = f32[2,640,1024]{2,1,0:T(8,128)} fusion(f32[2,1024]{1,0:T(2,128)S(1)} %bitcast.134, bf16[4096,2,1024]{2,1,0:T(2,128)(2,1)} %broadcast_select_fusion, f32[2,640,4096]{2,1,0:T(8,128)} %fusion.150, f32[2,4096]{1,0:T(2,128)S(1)} %convert_element_type.108), kind=kOutput, calls=%fused_computation.95 | convolution fusion | flops 10791157760 | bytes 43032576 | tf_op jit(solution)/shard_map/ecf,fed->ecd/dot_general | solution.py:142
  1248.0 8.9 gather_fusion.1
  1256.9 5.2 multiply_reduce_fusion.2
  1262.8 4.8 fusion.143
  1270.8 2.4 convolution_convert_fusion
  1274.3 13.6 fusion.153
  1288.0 67.6 %fusion.91 = bf16[512,16,64]{0,2,1:T(8,128)(2,1)} fusion(bf16[1024,16,64]{0,2,1:T(8,128)(2,1)S(1)} %bitcast.94, f32[16,512,1024]{2,1,0:T(8,128)} %fusion.153, f32[16,512,1024]{2,1,0:T(8,128)} %get-tuple-element.114, f32[16,512]{1,0:T(8,128)S(1)} %copy-done.49, pred[512,1024]{1,0:T(8,128)(4,1)} %get-tuple-element.110), kind=kOutput, calls=%fused_computation.105 | convolution fusion | flops 1166550016 | bytes 70811648 | tf_op jit(solution)/shard_map/hqk,khd->qhd/dot_general | solution.py:221
  1355.6 6.5 fusion.154
  1362.2 15.4 fusion.152
  1377.7 67.9 %fusion.88 = bf16[512,16,64]{0,2,1:T(8,128)(2,1)} fusion(bf16[1024,16,64]{0,2,1:T(8,128)(2,1)S(1)} %bitcast.95, f32[16,512,1024]{2,1,0:T(8,128)} %fusion.152, f32[16,512,1024]{2,1,0:T(8,128)} %get-tuple-element.116, f32[16,512]{1,0:T(8,128)S(1)} %copy-done.51, pred[512,1024]{1,0:T(8,128)(4,1)} %get-tuple-element.109), kind=kOutput, calls=%fused_computation.104 | convolution fusion | flops 1166550016 | bytes 70811648 | tf_op jit(solution)/shard_map/hqk,khd->qhd/dot_general | solution.py:221
  1445.5 3.1 pad_maximum_fusion.2
  1448.7 61.0 %fusion.19 = f32[16,64,1024]{2,1,0:T(8,128)} fusion(bf16[512,16,64]{0,2,1:T(8,128)(2,1)S(1)} %bitcast.104, f32[16,512,1024]{2,1,0:T(8,128)} %fusion.152, f32[16,512,1024]{2,1,0:T(8,128)} %get-tuple-element.116, f32[16,512]{1,0:T(8,128)S(1)} %copy-done.51, pred[512,1024]{1,0:T(8,128)(4,1)} %get-tuple-element.109), kind=kOutput, calls=%fused_computation.34 | convolution fusion | flops 1166025728 | bytes 72908800 | tf_op jit(solution)/shard_map/hqk,qhd->khd/dot_general | solution.py:223
  1509.6 60.4 %add_convert_fusion.2 = bf16[16,64,1024]{2,1,0:T(8,128)(2,1)} fusion(f32[16,64,1024]{2,1,0:T(8,128)} %fusion.19, bf16[512,16,64]{0,2,1:T(8,128)(2,1)S(1)} %bitcast.106, f32[16,512,1024]{2,1,0:T(8,128)} %fusion.153, f32[16,512,1024]{2,1,0:T(8,128)} %get-tuple-element.114, f32[16,512]{1,0:T(8,128)S(1)} %copy-done.49, pred[512,1024]{1,0:T(8,128)(4,1)} %get-tuple-element.110), kind=kOutput, calls=%fused_computation.85 | convolution fusion | flops 1168122880 | bytes 75005952 | tf_op jit(solution)/shard_map/hqk,qhd->khd/dot_general | solution.py:223
  1570.0 17.6 fusion.98
  1587.6 18.6 add_convert_fusion.1
  1606.3 14.7 fusion.135
  1622.5 11.7 fusion.140
  1634.3 4.8 convert_reduce_fusion.1
  1639.1 2.3 fusion.73
  1641.4 37.9 %all-reduce.17 = (f32[1024]{0:T(1024)S(1)}, f32[1024]{0:T(1024)S(1)}, f32[1024]{0:T(1024)S(1)}, f32[1024]{0:T(1024)S(1)}, f32[1024]{0:T(1024)S(1)}, /*index=5*/f32[1024]{0:T(1024)S(1)}, f32[1024]{0:T(1024)S(1)}) all-reduce(f32[1024]{0:T(1024)S(1)} %get-tuple-element.77, ...), channel_id=2, replica_groups=mesh['dp'=4,'fsdp'=8] {'dp','fsdp'}, use_global_device_ids=true, to_apply=%region_19.20.clone | all-reduce | flops 7168 | bytes 57344
  1683.4 6.3 add_add_fusion.2
  1691.2 2.3 constant_dynamic-slice_fusion
  1693.5 2.3 copy.86
  1695.8 54.4 %reduce-scatter.12.cloned.1.call-done = f32[32,1024]{1,0:T(8,128)} async-done(((f32[1024,1024]{1,0:T(8,128)}), f32[32,1024]{1,0:T(8,128)}) %reduce-scatter.12.cloned.1.call-update) | async-done | bytes 131088 | tf_op jit(solution)/shard_map/reduce_scatter | solution.py:249
  1750.2 160.4 %reduce-scatter.10.cloned.1.call-done = f32[32,3072]{1,0:T(8,128)} async-done(((f32[1024,3072]{1,0:T(8,128)}), f32[32,3072]{1,0:T(8,128)}) %reduce-scatter.10.cloned.1.call-update) | async-done | bytes 393232 | tf_op jit(solution)/shard_map/reduce_scatter | solution.py:248
  (241 shorter events, 45.7 us)
Async XLA Ops:
  7.2 115.9 %all-gather.6.cloned.1.call-start = ((), (), s32[]{:S(2)}) async-start(), calls=%async_computation.5 | async-start | bytes 6488064 | tf_op jit(solution)/shard_map/all_gather | solution.py:53
  7.9 232.2 %all-gather.8.cloned.1.call-start = ((), (), s32[]{:S(2)}) async-start(), calls=%async_computation.6 | async-start | bytes 2162688 | tf_op jit(solution)/shard_map/all_gather | solution.py:54
  8.7 249.9 %all-gather.10.cloned.1.call-start = ((), (), s32[]{:S(2)}) async-start(), calls=%async_computation.7 | async-start | bytes 17301504 | tf_op jit(solution)/shard_map/all_gather | solution.py:109
  10.9 363.6 %all-gather.12.cloned.1.call-start = ((), (), s32[]{:S(2)}) async-start(), calls=%async_computation.8 | async-start | bytes 17301504 | tf_op jit(solution)/shard_map/all_gather | solution.py:149
  12.9 1608.2 %reduce-scatter.18.cloned.1.call-start = ((), (), s32[]{:S(2)}) async-start(), calls=%async_computation.13 | async-start | bytes 540672
  22.8 8.7 copy-start.63
  22.8 8.9 copy-start.64
  22.9 9.1 copy-start.65
  22.9 9.3 copy-start.66
  22.9 9.6 copy-start.67
  22.9 9.8 copy-start.68
  22.9 10.0 copy-start.69
  22.9 58.7 %copy-start.60 = (bf16[2,128]{1,0:T(2,128)(2,1)S(1)}, bf16[2,128]{1,0:T(2,128)(2,1)}, u32[]{:S(2)}) copy-start(bf16[2,128]{1,0:T(2,128)(2,1)} %param.30) | copy-start | bytes 1540
  22.9 98.5 %copy-start.55 = (s32[1,1024]{1,0:T(1,128)S(1)}, s32[1,1024]{1,0:T(1,128)}, u32[]{:S(2)}) copy-start(s32[1,1024]{1,0:T(1,128)} %param.18) | copy-start | bytes 12292
  28.0 95.1 %copy-start.8 = (bf16[1024,1024]{1,0:T(8,128)(2,1)S(1)}, bf16[1024,1024]{1,0:T(8,128)(2,1)}, u32[]{:S(2)}) copy-start(bf16[1024,1024]{1,0:T(8,128)(2,1)} %param.17) | copy-start | bytes 6291460
  31.4 1658.3 %reduce-scatter.16.cloned.1.call-start = ((), (), s32[]{:S(2)}) async-start(), calls=%async_computation.12 | async-start | bytes 2162688
  76.6 56.8 %copy-start.40 = (f32[1024]{0:T(1024)}, f32[1024]{0:T(1024)S(1)}, u32[]{:S(2)}) copy-start(f32[1024]{0:T(1024)S(1)} %convert_element_type.95) | copy-start | bytes 12292
  76.6 170.7 %copy-start.32 = (f32[1024]{0:T(1024)}, f32[1024]{0:T(1024)S(1)}, u32[]{:S(2)}) copy-start(f32[1024]{0:T(1024)S(1)} %convert_element_type.104) | copy-start | bytes 12292
  76.6 56.8 %copy-start.58 = (f32[1024]{0:T(1024)}, f32[1024]{0:T(1024)S(1)}, u32[]{:S(2)}) copy-start(f32[1024]{0:T(1024)S(1)} %convert_element_type.96) | copy-start | bytes 12292
  78.6 54.9 %copy-start.36 = (f32[1024]{0:T(1024)}, f32[1024]{0:T(1024)S(1)}, u32[]{:S(2)}) copy-start(f32[1024]{0:T(1024)S(1)} %broadcast_multiply_fusion.1) | copy-start | bytes 12292
  81.6 51.9 %copy-start.42 = (f32[1024]{0:T(1024)}, f32[1024]{0:T(1024)S(1)}, u32[]{:S(2)}) copy-start(f32[1024]{0:T(1024)S(1)} %fusion.105) | copy-start | bytes 12292
  140.3 24.4 %copy-start.2 = (bf16[1024,1024]{0,1:T(8,128)(2,1)}, bf16[1024,1024]{0,1:T(8,128)(2,1)S(1)}, u32[]{:S(2)}) copy-start(bf16[1024,1024]{0,1:T(8,128)(2,1)S(1)} %copy.77) | copy-start | bytes 6291460
  142.5 22.2 %copy-start.13 = (bf16[512,1024]{0,1:T(8,128)(2,1)}, bf16[512,1024]{0,1:T(8,128)(2,1)S(1)}, u32[]{:S(2)}) copy-start(bf16[512,1024]{0,1:T(8,128)(2,1)S(1)} %copy.76) | copy-start | bytes 3145732
  149.1 15.5 copy-start.19
  164.7 14.2 copy-start.16
  178.9 25.7 %copy-start.4 = (bf16[1024,1024]{0,1:T(8,128)(2,1)S(1)}, bf16[1024,1024]{0,1:T(8,128)(2,1)}, u32[]{:S(2)}) copy-start(bf16[1024,1024]{0,1:T(8,128)(2,1)} %copy.75) | copy-start | bytes 6291460
  178.9 25.7 %copy-start.20 = (pred[512,1024]{1,0:T(8,128)(4,1)S(1)}, pred[512,1024]{1,0:T(8,128)(4,1)}, u32[]{:S(2)}) copy-start(pred[512,1024]{1,0:T(8,128)(4,1)} %get-tuple-element.109) | copy-start | bytes 1572868
  204.6 17.7 copy-start.48
  204.6 17.6 copy-start.50
  204.6 17.6 copy-start.17
  258.6 115.9 %copy-start.12 = (bf16[1280,1024]{1,0:T(8,128)(2,1)S(1)}, bf16[1280,1024]{1,0:T(8,128)(2,1)}, u32[]{:S(2)}) copy-start(bf16[1280,1024]{1,0:T(8,128)(2,1)} %gather_fusion.2) | copy-start | bytes 7864324
  406.2 1285.0 %all-reduce.21.cloned.1.call-start = ((), (), s32[]{:S(2)}) async-start(), calls=%async_computation.14 | async-start | bytes 67108864
  478.4 1215.1 %reduce-scatter.14.cloned.1.call-start = ((), (), s32[]{:S(2)}) async-start(), calls=%async_computation.11 | async-start | bytes 34603008 | tf_op jit(solution)/shard_map/reduce_scatter | solution.py:179
  503.8 1246.4 %reduce-scatter.12.cloned.1.call-start = ((), (), s32[]{:S(2)}) async-start(), calls=%async_computation.10 | async-start | bytes 4325376 | tf_op jit(solution)/shard_map/reduce_scatter | solution.py:249
  504.8 1.9 collective-permute-start
  509.6 30.0 %collective-permute-start.1 = (bf16[256,2,1024]{2,1,0:T(2,128)(2,1)S(1)}, bf16[256,2,1024]{2,1,0:T(2,128)(2,1)}, u32[]{:S(2)}, u32[]{:S(2)}) collective-permute-start(bf16[256,2,1024]{2,1,0:T(2,128)(2,1)S(1)} %broadcast_select_fusion.4), channel_id=1, source_target_pairs={{0,2},{1,3},{2,0},{3,1},{4,6},{5,7},{6,4},{7,5},{8,10},{9,11},{10,... | collective-permute-start | bytes 3145736 | tf_op jit(solution)/shard_map/ppermute | solution.py:17
  545.4 105.5 %collective-permute-start.2 = (bf16[512,2,1024]{2,1,0:T(2,128)(2,1)S(1)}, bf16[512,2,1024]{2,1,0:T(2,128)(2,1)}, u32[]{:S(2)}, u32[]{:S(2)}) collective-permute-start(bf16[512,2,1024]{2,1,0:T(2,128)(2,1)S(1)} %broadcast_select_fusion.3), channel_id=1, source_target_pairs={{0,4},{1,5},{2,6},{3,7},{4,0},{5,1},{6,2},{7,3},{8,12},{9,13},{10,... | collective-permute-start | bytes 6291464 | tf_op jit(solution)/shard_map/ppermute | solution.py:17
  662.2 144.1 %collective-permute-start.3 = (bf16[1024,2,1024]{2,1,0:T(2,128)(2,1)}, bf16[1024,2,1024]{2,1,0:T(2,128)(2,1)}, u32[]{:S(2)}, u32[]{:S(2)}) collective-permute-start(bf16[1024,2,1024]{2,1,0:T(2,128)(2,1)} %broadcast_select_fusion.2), channel_id=1, source_target_pairs={{0,8},{1,9},{2,10},{3,11},{4,12},{5,13},{6,14},{7,15},{8,0},{9,1},... | collective-permute-start | bytes 12582920 | tf_op jit(solution)/shard_map/ppermute | solution.py:17
  664.2 185.0 %copy-start.61 = (bf16[2,32]{1,0:T(2,128)(2,1)S(1)}, bf16[2,32]{1,0:T(2,128)(2,1)}, u32[]{:S(2)}) copy-start(bf16[2,32]{1,0:T(2,128)(2,1)} %param.32) | copy-start | bytes 388
  664.3 223.5 %copy-start.57 = (s32[1024,1]{0,1:T(1,128)S(1)}, s32[1024,1]{0,1:T(1,128)}, u32[]{:S(2)}) copy-start(s32[1024,1]{0,1:T(1,128)} %copy-done.56) | copy-start | bytes 12292
  847.8 266.0 %collective-permute-start.4 = (bf16[2048,2,1024]{2,1,0:T(2,128)(2,1)}, bf16[2048,2,1024]{2,1,0:T(2,128)(2,1)}, u32[]{:S(2)}, u32[]{:S(2)}) collective-permute-start(bf16[2048,2,1024]{2,1,0:T(2,128)(2,1)} %broadcast_select_fusion.1), channel_id=1, source_target_pairs={{0,16},{1,17},{2,18},{3,19},{4,20},{5,21},{6,22},{7,23},{8,24},{9,... | collective-permute-start | bytes 25165832 | tf_op jit(solution)/shard_map/ppermute | solution.py:17
  1247.9 8.9 copy-start.31
  1247.9 8.9 copy-start.33
  1247.9 8.9 copy-start.35
  1273.4 88.8 %copy-start.24 = (bf16[512,1024]{0,1:T(8,128)(2,1)}, bf16[512,1024]{0,1:T(8,128)(2,1)S(1)}, u32[]{:S(2)}) copy-start(bf16[512,1024]{0,1:T(8,128)(2,1)S(1)} %get-tuple-element.108) | copy-start | bytes 3145732
  1274.3 13.6 copy-start.3
  1274.3 13.6 copy-start.49
  1362.1 548.4 %reduce-scatter.10.cloned.1.call-start = ((), (), s32[]{:S(2)}) async-start(), calls=%async_computation.9 | async-start | bytes 12976128 | tf_op jit(solution)/shard_map/reduce_scatter | solution.py:248
  1362.2 15.5 copy-start.51
  1377.7 71.0 %copy-start.14 = (bf16[512,1024]{0,1:T(8,128)(2,1)S(1)}, bf16[512,1024]{0,1:T(8,128)(2,1)}, u32[]{:S(2)}) copy-start(bf16[512,1024]{0,1:T(8,128)(2,1)} %copy-done.13) | copy-start | bytes 3145732
  1448.7 61.0 %copy-start.15 = (bf16[512,1024]{0,1:T(8,128)(2,1)S(1)}, bf16[512,1024]{0,1:T(8,128)(2,1)}, u32[]{:S(2)}) copy-start(bf16[512,1024]{0,1:T(8,128)(2,1)} %copy.78) | copy-start | bytes 3145732
  1509.6 60.4 %copy-start.21 = (pred[512,1024]{1,0:T(8,128)(4,1)S(1)}, pred[512,1024]{1,0:T(8,128)(4,1)}, u32[]{:S(2)}) copy-start(pred[512,1024]{1,0:T(8,128)(4,1)} %get-tuple-element.109) | copy-start | bytes 1572868
  1570.0 17.6 copy-start.18
  1587.6 18.7 copy-start.9
  1587.6 18.7 copy-start.37
  1587.6 18.7 copy-start.41
  1587.6 18.7 copy-start.43
  1587.6 18.7 copy-start.59
  1622.5 11.7 copy-start.45
  1622.5 11.8 copy-start.22
  1622.5 11.8 copy-start.28
  1622.5 11.8 copy-start.29
  1634.2 7.2 copy-start.52
  1634.2 49.2 %copy-start.39 = (f32[1024]{0:T(1024)S(1)}, f32[1024]{0:T(1024)}, u32[]{:S(2)}) copy-start(f32[1024]{0:T(1024)} %copy-done.38) | copy-start | bytes 12292
  (21 other events, 78.1 us)
Sparse Core Ops, SparseCore 0:
  11.0 72.0 all-gather.5
  86.1 55.7 all-gather.7
  144.9 113.6 all-gather.9
  261.5 112.9 all-gather.11
  376.6 132.2 reduce-scatter.17
  511.1 164.8 reduce-scatter.15
  682.3 563.5 all-reduce.20
  1248.3 359.9 reduce-scatter.13
  1611.2 138.9 reduce-scatter.11
  1757.7 152.8 reduce-scatter.9
